TPU v7x, 32 devices: a whole 2x2x4 slice. The times are simulated.
32 devices in a mesh: ctx: 16 (over z, y, core), wa: 2 (over x).
Axes of the slice: x: 2, y: 2, z: 4, core: 2. Of those that a mesh axis runs over, the one named last changes fastest.
Arguments:
- query_in: bfloat16 [2, 4096, 512], P('wa', 'ctx'), may hold values from -6 to 6
- content_in: bfloat16 [2, 4096, 512], P('wa', 'ctx'), may hold values from -6 to 6
- encoder_in: bfloat16 [2, 4096, 512], P('wa', 'ctx'), may hold values from -6 to 6
- out_grad: bfloat16 [2, 4096, 512], P('wa', 'ctx'), may hold values from -6 to 6
- document_lengths: int32 [2, 4], P('wa'), may hold values from 1 to 2048, 4096 in all within a row
- key_ranks: int32 [2, 4096], P('wa'), may hold values from 0 to 15
- query_limits: int32 [2, 4096], P('wa'), may hold values from 1 to 16
- self_query_weight: bfloat16 [512, 512], P('wa'), may hold values from -0.25 to 0.25
- self_query_bias: bfloat16 [512], P('wa'), may hold values from -3 to 3
- self_key_weight: bfloat16 [512, 512], P('wa'), may hold values from -0.25 to 0.25
- self_value_weight: bfloat16 [512, 512], P('wa'), may hold values from -0.25 to 0.25
- self_value_bias: bfloat16 [512], P('wa'), may hold values from -0.29882812 to 0.29882812
- self_out_weight: bfloat16 [512, 512], P('wa'), may hold values from -3 to 3
- self_out_bias: bfloat16 [512], P('wa'), may hold values from -3 to 3
- norm_one_gain: bfloat16 [512], P('wa'), may hold values from 0.099609375 to 1.8984375
- norm_one_shift: bfloat16 [512], P('wa'), may hold values from -2 to 2
- cross_query_weight: bfloat16 [512, 512], P('wa'), may hold values from -0.25 to 0.25
- cross_query_bias: bfloat16 [512], P('wa'), may hold values from -3 to 3
- cross_key_weight: bfloat16 [512, 512], P('wa'), may hold values from -0.25 to 0.25
- cross_value_weight: bfloat16 [512, 512], P('wa'), may hold values from -0.25 to 0.25
- cross_value_bias: bfloat16 [512], P('wa'), may hold values from -0.29882812 to 0.29882812
- cross_out_weight: bfloat16 [512, 512], P('wa'), may hold values from -3 to 3
- cross_out_bias: bfloat16 [512], P('wa'), may hold values from -3 to 3
- norm_two_gain: bfloat16 [512], P('wa'), may hold values from 0.099609375 to 1.8984375
- norm_two_shift: bfloat16 [512], P('wa'), may hold values from -2 to 2
- expand_weight: bfloat16 [512, 2048], P('wa'), may hold values from -0.25 to 0.25
- expand_bias: bfloat16 [2048], P('wa'), may hold values from -2 to 2
- shrink_weight: bfloat16 [2048, 512], P('wa'), may hold values from -0.125 to 0.125
- shrink_bias: bfloat16 [512], P('wa'), may hold values from -2 to 2
- norm_three_gain: bfloat16 [512], P('wa'), may hold values from 0.099609375 to 1.8984375
- norm_three_shift: bfloat16 [512], P('wa'), may hold values from -2 to 2
Outputs:
- layer_out: float32 [2, 4096, 512], P('wa', 'ctx')
- query_grad: float32 [2, 4096, 512], P('wa', 'ctx')
- content_grad: float32 [2, 4096, 512], P('wa', 'ctx')
- encoder_grad: float32 [2, 4096, 512], P('wa', 'ctx')
- grad_self_query_weight: float32 [512, 512], P('wa')
- grad_self_query_bias: float32 [512], P('wa')
- grad_self_key_weight: float32 [512, 512], P('wa')
- grad_self_value_weight: float32 [512, 512], P('wa')
- grad_self_value_bias: float32 [512], P('wa')
- grad_self_out_weight: float32 [512, 512], P('wa')
- grad_self_out_bias: float32 [512], P('wa')
- grad_norm_one_gain: float32 [512], P('wa')
- grad_norm_one_shift: float32 [512], P('wa')
- grad_cross_query_weight: float32 [512, 512], P('wa')
- grad_cross_query_bias: float32 [512], P('wa')
- grad_cross_key_weight: float32 [512, 512], P('wa')
- grad_cross_value_weight: float32 [512, 512], P('wa')
- grad_cross_value_bias: float32 [512], P('wa')
- grad_cross_out_weight: float32 [512, 512], P('wa')
- grad_cross_out_bias: float32 [512], P('wa')
- grad_norm_two_gain: float32 [512], P('wa')
- grad_norm_two_shift: float32 [512], P('wa')
- grad_expand_weight: float32 [512, 2048], P('wa')
- grad_expand_bias: float32 [2048], P('wa')
- grad_shrink_weight: float32 [2048, 512], P('wa')
- grad_shrink_bias: float32 [512], P('wa')
- grad_norm_three_gain: float32 [512], P('wa')
- grad_norm_three_shift: float32 [512], P('wa')
Inputs may be any that keep to these rules, and one draw needn't show every extreme that they name: `document_lengths`: each row gives the 4 document lengths of one packed sequence in order; they sum to 4096, and the longest is exactly 2048.
All inputs are finite; a program needn't handle non-finite values.
Results may differ from a plain program's by a relative error of at most 0.03.
Values may be sent and summed in bfloat16 or wider, within the bound.
A program may use at most 320 MiB of HBM per device.

v0:
```python
import functools
import jax
import jax.numpy as jnp
from jax import lax
from jax.experimental import pallas as pl
from jax.experimental.pallas import tpu as pltpu
from jax.sharding import Mesh
from jax.sharding import PartitionSpec as P

PLANE = 4
DOCLEN = 2048
EPSILON = 1e-05
ROOT_HALF = 0.7071067811865476
INV_ROOT_TWO_PI = 0.3989422804014327

NEGATIVE = -1e29
HIDE = -(2.0 ** 100)
BLOCK = 256
WIDE = 512
STAT = 40


def dot(a, b, ca, cb):
    return lax.dot_general(a, b, (((ca,), (cb,)), ((), ())), preferred_element_type=jnp.float32)


def left_half(shape):
    return lax.broadcasted_iota(jnp.int32, shape, 1) < 64


def spans(lens_ref, first, count):
    low, high, total = 0, 0, 0
    for d in range(lens_ref.shape[1]):
        begin = total
        total = total + lens_ref[0, d]
        low = jnp.where(begin <= first, begin, low)
        high = jnp.where(begin <= first + count - 1, total, high)
    return low, high


def openings(lens_ref, places):
    total, found = 0, places == 0
    for d in range(lens_ref.shape[1] - 1):
        total = total + lens_ref[0, d]
        found = jnp.logical_or(found, places == total)
    return found


def over_blocks(low, high, first, size, step, carry, ranked):
    begin, end = low // size, (high + size - 1) // size
    own = first // size
    skip = 1 if ranked else 0

    def body(index, carry):
        if ranked:
            index = index + jnp.where(index >= own, 1, 0)
        return step(pl.multiple_of(index * size, size), carry)

    carry = lax.fori_loop(begin, end - skip, body, carry)
    if ranked:
        carry = step(pl.multiple_of(own * size, size), carry, True)
    return carry


def forward_kernel(ranked, lens_ref, own_ref, q_ref, qm_ref, k_ref, v_ref, km_ref, o_ref, lse_ref):
    rows = q_ref.shape[0]
    base = own_ref[0] * rows
    half = left_half((BLOCK, 128))
    khalf = left_half((WIDE, 128))
    one = jnp.ones((WIDE, 128), jnp.bfloat16)

    def one_block(block, _):
        start = pl.multiple_of(block * BLOCK, BLOCK)
        first = base + start
        low, high = spans(lens_ref, first, BLOCK)
        q = q_ref[pl.ds(start, BLOCK), :]
        qm = qm_ref[pl.ds(start, BLOCK), :]
        queries = (jnp.where(half, q, qm), jnp.where(half, qm, q))

        def step(at, carry, diagonal=False):
            k = k_ref[pl.ds(at, WIDE), :]
            v = v_ref[pl.ds(at, WIDE), :]
            km = km_ref[pl.ds(at, WIDE), :]
            keys = (jnp.where(khalf, k, km), jnp.where(khalf, km, k))
            values = (jnp.where(khalf, v, one), jnp.where(khalf, one, v))
            scores = [dot(queries[h], keys[h], 1, 1) for h in (0, 1)]
            if diagonal:
                place = first + lax.broadcasted_iota(jnp.int32, (BLOCK, WIDE), 0)
                other = at + lax.broadcasted_iota(jnp.int32, (BLOCK, WIDE), 1)
                column = first + lax.broadcasted_iota(jnp.int32, (BLOCK, 1), 0)
                banned = jnp.where(openings(lens_ref, column), -1, place) == other
                scores = [jnp.where(banned, HIDE, s) for s in scores]
            out = []
            for h in (0, 1):
                peak, acc = carry[h]
                new = jnp.maximum(peak, jnp.max(scores[h], axis=1, keepdims=True))
                p = jnp.exp(scores[h] - new).astype(jnp.bfloat16)
                acc = acc * jnp.exp(peak - new) + dot(p, values[h], 1, 0)
                out.append((new, acc))
            return tuple(out)

        empty = (jnp.full((BLOCK, 1), NEGATIVE, jnp.float32), jnp.zeros((BLOCK, 128), jnp.float32))
        (peak0, acc0), (peak1, acc1) = over_blocks(low, high, first, WIDE, step, (empty, empty), ranked)
        total = jnp.where(half, acc1, acc0)
        mixed = jnp.where(half, acc0, acc1)
        o_ref[pl.ds(start, BLOCK), :] = mixed / pltpu.roll(total, 64, 1)
        lse_ref[pl.ds(start, BLOCK), :] = jnp.where(half, peak1, peak0) + jnp.log(total)
        return 0

    lax.fori_loop(0, rows // BLOCK, one_block, 0)


def attend_forward(ranked, lens, own, q, qm, k, v, km):
    rows = q.shape[0]
    whole = pl.BlockSpec(memory_space=pltpu.VMEM)
    smem = pl.BlockSpec(memory_space=pltpu.SMEM)
    return pl.pallas_call(
        functools.partial(forward_kernel, ranked),
        out_shape=(jax.ShapeDtypeStruct((rows, 128), jnp.float32),) * 2,
        in_specs=[smem, smem] + [whole] * 5,
        out_specs=(whole, whole),
        compiler_params=pltpu.CompilerParams(vmem_limit_bytes=56 << 20),
    )(lens, own, q, qm, k, v, km)


def with_stat(marks, stat, lane, at):
    high = stat.astype(jnp.bfloat16)
    rest = stat - high.astype(jnp.float32)
    middle = rest.astype(jnp.bfloat16)
    tail = (rest - middle.astype(jnp.float32)).astype(jnp.bfloat16)
    side = jnp.where(lane == at, high, jnp.where(lane == at + 1, middle, jnp.where(lane == at + 2, tail, marks)))
    return side


def backward_kernel(ranked, lens_ref, own_ref, q_ref, qm_ref, k_ref, v_ref, km_ref, o_ref, lse_ref, do_ref,
                    dq_ref, dk_ref, dv_ref):
    rows = q_ref.shape[0]
    base = own_ref[0] * rows
    half = left_half((BLOCK, 128))
    lane = lax.broadcasted_iota(jnp.int32, (BLOCK, 128), 1)
    one = jnp.ones((BLOCK, 128), jnp.bfloat16)
    zero = jnp.zeros((BLOCK, 128), jnp.bfloat16)

    def clear(index, _):
        at = pl.multiple_of(index * BLOCK, BLOCK)
        dk_ref[pl.ds(at, BLOCK), :] = jnp.zeros((BLOCK, 128), jnp.float32)
        dv_ref[pl.ds(at, BLOCK), :] = jnp.zeros((BLOCK, 128), jnp.float32)
        return 0

    lax.fori_loop(0, k_ref.shape[0] // BLOCK, clear, 0)

    def one_block(block, _):
        start = pl.multiple_of(block * BLOCK, BLOCK)
        first = base + start
        low, high = spans(lens_ref, first, BLOCK)
        here = pl.ds(start, BLOCK)
        q, qm, do, lse = q_ref[here, :], qm_ref[here, :], do_ref[here, :], lse_ref[here, :]
        shared = do.astype(jnp.float32) * o_ref[here, :]
        delta0 = jnp.sum(jnp.where(half, shared, 0.0), axis=1, keepdims=True)
        delta1 = jnp.sum(jnp.where(half, 0.0, shared), axis=1, keepdims=True)
        side = with_stat(qm, lse, lane % 64, STAT)
        queries = (jnp.where(half, q, side), jnp.where(half, side, q))
        side = with_stat(zero, -jnp.where(half, delta1, delta0), lane % 64, STAT)
        grads = (jnp.where(half, do, side), jnp.where(half, side, do))

        def step(at, carry, diagonal=False):
            there = pl.ds(at, BLOCK)
            k, v, km = k_ref[there, :], v_ref[there, :], km_ref[there, :]
            keys = (jnp.where(half, k, km), jnp.where(half, km, k))
            values = (jnp.where(half, v, one), jnp.where(half, one, v))
            scores = [dot(keys[h], queries[h], 1, 1) for h in (0, 1)]
            if diagonal:
                other = first + lax.broadcasted_iota(jnp.int32, (BLOCK, BLOCK), 0)
                row = first + lax.broadcasted_iota(jnp.int32, (1, BLOCK), 1)
                banned = other == jnp.where(openings(lens_ref, row), -1, row)
                scores = [jnp.where(banned, HIDE, s) for s in scores]
            dvs, dks, dqs = [], [], []
            for h in (0, 1):
                p = jnp.exp(scores[h])
                dp = dot(values[h], grads[h], 1, 1)
                ds = (p * dp).astype(jnp.bfloat16)
                dvs.append(dot(p.astype(jnp.bfloat16), do, 1, 0))
                dks.append(dot(ds, q, 1, 0))
                dqs.append(dot(ds, k, 0, 0))
            dv_ref[there, :] += jnp.where(half, dvs[0], dvs[1])
            dk_ref[there, :] += jnp.where(half, dks[0], dks[1])
            return carry + jnp.where(half, dqs[0], dqs[1])

        dq = over_blocks(low, high, first, BLOCK, step, jnp.zeros((BLOCK, 128), jnp.float32), ranked)
        dq_ref[here, :] = (dq * 0.125).astype(dq_ref.dtype)
        return 0

    lax.fori_loop(0, rows // BLOCK, one_block, 0)


def attend_backward(ranked, lens, own, q, qm, k, v, km, o, lse, do):
    rows, keys = q.shape[0], k.shape[0]
    whole = pl.BlockSpec(memory_space=pltpu.VMEM)
    smem = pl.BlockSpec(memory_space=pltpu.SMEM)
    return pl.pallas_call(
        functools.partial(backward_kernel, ranked),
        out_shape=(jax.ShapeDtypeStruct((rows, 128), jnp.bfloat16),) + (jax.ShapeDtypeStruct((keys, 128), jnp.float32),) * 2,
        in_specs=[smem, smem] + [whole] * 8,
        out_specs=(whole, whole, whole),
        compiler_params=pltpu.CompilerParams(vmem_limit_bytes=56 << 20),
    )(lens, own, q, qm, k, v, km, o, lse, do)


def mark_tables(lengths, ranks, limits, offset, rows, ranked):
    total = ranks.shape[0]
    docs = lengths.shape[0]
    ends = jnp.stack([jnp.sum(lengths[: d + 1]) for d in range(docs)])
    begins = jnp.stack([jnp.sum(lengths[:d]) for d in range(docs)])
    place = lax.broadcasted_iota(jnp.int32, (total, 64), 0)
    lane = lax.broadcasted_iota(jnp.int32, (total, 64), 1)
    doc = jnp.zeros((total, 1), jnp.int32)
    is_open = jnp.zeros((total, 1), bool)
    for d in range(docs):
        doc = doc + (place[:, :1] >= ends[d]).astype(jnp.int32)
        is_open = jnp.logical_or(is_open, place[:, :1] == begins[d])
    rank = jnp.where(is_open, 0, ranks[:, None] + 1)
    key_marks = jnp.where(lane == doc, 1.0, 0.0)
    if ranked:
        key_marks = key_marks + jnp.where(lane == rank + 16, 1.0, 0.0)
    key_marks = key_marks - jnp.where(jnp.logical_and(lane >= STAT, lane < STAT + 3), 1.0, 0.0)
    hide = jnp.where(jnp.logical_and(lane < docs, lane != doc), HIDE, 0.0)
    if ranked:
        hide = hide + jnp.where(jnp.logical_and(lane >= 16, jnp.logical_and(lane < 33, lane - 17 >= limits[:, None])), HIDE, 0.0)
    query_marks = lax.dynamic_slice_in_dim(hide, offset, rows, 0)
    both = lambda m: jnp.concatenate([m, m], axis=1).astype(jnp.bfloat16)
    return both(key_marks), both(query_marks)


def matmul(left, right):
    return jnp.dot(left, right, preferred_element_type=jnp.float32)


def left_product(left, right):
    return jnp.einsum("ta,tb->ab", left, right, preferred_element_type=jnp.float32)


def right_product(left, right):
    return jnp.einsum("ta,ba->tb", left, right, preferred_element_type=jnp.float32)


def column_sum(value):
    return jnp.sum(value.astype(jnp.float32), axis=0)


def gelu_slope(value):
    cumulative = 0.5 * (1.0 + lax.erf(value * ROOT_HALF))
    return cumulative + value * jnp.exp(-0.5 * value * value) * INV_ROOT_TWO_PI


def norm_forward(value, gain_row, shift_row):
    middle = jnp.mean(value, axis=-1, keepdims=True)
    centred = value - middle
    spread = jnp.mean(centred * centred, axis=-1, keepdims=True)
    inverse = lax.rsqrt(spread + EPSILON)
    normed = centred * inverse
    return (normed * gain_row + shift_row, normed, inverse)


def norm_backward(incoming, normed, inverse, gain_row):
    scaled = incoming * gain_row
    centred = (
        scaled
        - jnp.mean(scaled, axis=-1, keepdims=True)
        - normed * jnp.mean(scaled * normed, axis=-1, keepdims=True)
    )
    return (inverse * centred, jnp.sum(incoming * normed, axis=0), jnp.sum(incoming, axis=0))


MESH = pl.DeviceIdType.MESH
ANY = pl.BlockSpec(memory_space=pltpu.HBM)
VMEM = pl.BlockSpec(memory_space=pltpu.VMEM)
SMEM = pl.BlockSpec(memory_space=pltpu.SMEM)
DMA = pltpu.SemaphoreType.DMA


def across(place, offset):
    if offset == 1:
        return place + 1 - 2 * lax.rem(place, 2)
    if offset == 2:
        return lax.rem(place + 2, 4)
    return 3 - place


def remote(src, dst, sends, recvs, where):
    return pltpu.make_async_remote_copy(
        src_ref=src, dst_ref=dst, send_sem=sends, recv_sem=recvs, device_id=where, device_id_type=MESH)


def greet(grp_count, wa_count, plane=True, groups=True, rows=True):
    barrier = pltpu.get_barrier_semaphore()
    grp, pln, wa = lax.axis_index("grp"), lax.axis_index("pln"), lax.axis_index("wa")

    def hello(where):
        pl.semaphore_signal(barrier, inc=1, device_id=where, device_id_type=MESH)

    count = 0
    if plane:
        for offset in (1, 2, 3):
            hello({"pln": across(pln, offset)})
        count += 3
    if rows:
        for offset in range(1, wa_count):
            hello({"wa": lax.rem(wa + offset, wa_count)})
        count += wa_count - 1
    if groups:
        @pl.when(grp > 0)
        def _():
            hello({"grp": grp - 1})

        @pl.when(grp < grp_count - 1)
        def _():
            hello({"grp": grp + 1})

        count = count + jnp.where(grp > 0, 1, 0) + jnp.where(grp < grp_count - 1, 1, 0)
    pl.semaphore_wait(barrier, count)


class Rows:
    def __init__(self, shard, full, sems, index, wa_count):
        self.shard, self.full, self.sems, self.index, self.wa_count = shard, full, sems, index, wa_count
        self.size = shard.shape[0]
        self.half = self.size // 2
        self.wa, self.pln = lax.axis_index("wa"), lax.axis_index("pln")
        self.core = lax.rem(self.pln, 2)

    def part(self, owner, core):
        return pl.ds(pl.multiple_of(owner * self.size + core * self.half, 16), self.half)

    def keep(self):
        own = pl.ds(pl.multiple_of(self.wa * self.size, 16), self.size)
        return pltpu.make_async_copy(self.shard, self.full.at[own], self.sems.at[0, self.index, 0])

    def push(self, offset):
        mine = pl.ds(pl.multiple_of(self.core * self.half, 16), self.half)
        return remote(self.shard.at[mine], self.full.at[self.part(self.wa, self.core)],
                      self.sems.at[1, self.index, offset - 1], self.sems.at[2, self.index, offset - 1],
                      {"wa": lax.rem(self.wa + offset, self.wa_count)})

    def hand(self, offset):
        owner = lax.rem(self.wa + self.wa_count - offset, self.wa_count)
        spot = self.full.at[self.part(owner, self.core)]
        return remote(spot, spot, self.sems.at[3, self.index, offset - 1], self.sems.at[4, self.index, offset - 1],
                      {"pln": across(self.pln, 1)})

    def begin(self):
        self.keep().start()
        for offset in range(1, self.wa_count):
            self.push(offset).start()

    def pass_on(self):
        for offset in range(1, self.wa_count):
            self.push(offset).wait_recv()
            self.hand(offset).start()

    def arrived(self):
        self.keep().wait()
        for offset in range(1, self.wa_count):
            self.hand(offset).wait_recv()

    def finish(self):
        for offset in range(1, self.wa_count):
            self.push(offset).wait_send()
            self.hand(offset).wait_send()


class Line:
    def __init__(self, full, sems, grp_count, reach, block):
        self.full, self.sems, self.count, self.reach, self.block = full, sems, grp_count, reach, block
        self.grp = lax.axis_index("grp")

    def rows(self, owner, block):
        return pl.ds(pl.multiple_of((owner * PLANE + block) * self.block, 16), self.block)

    def copy(self, side, step, block, source=None):
        toward = 1 if side == 0 else -1
        owner = self.grp - toward * (step - 1)
        spot = self.full.at[self.rows(owner, block)]
        return remote(spot if source is None else source, spot, self.sems.at[0, side, step - 1, block],
                      self.sems.at[1, side, step - 1, block], {"grp": self.grp + toward})

    def sends(self, side, step):
        if side == 0:
            return jnp.logical_and(self.grp - step + 1 >= 0, self.grp + 1 < self.count)
        return jnp.logical_and(self.grp + step - 1 < self.count, self.grp - 1 >= 0)

    def receives(self, side, step):
        return self.grp - step >= 0 if side == 0 else self.grp + step < self.count

    def send(self, step, block, source=None):
        for side in (0, 1):
            @pl.when(self.sends(side, step))
            def _():
                self.copy(side, step, block, source).start()

    def arrival(self, side, step, block):
        toward = 1 if side == 0 else -1
        spot = self.full.at[self.rows(self.grp - toward * step, block)]
        return remote(spot, spot, self.sems.at[0, side, step - 1, block], self.sems.at[1, side, step - 1, block],
                      {"grp": self.grp - toward})

    def forward(self, step):
        for block in range(PLANE):
            for side in (0, 1):
                @pl.when(self.receives(side, step))
                def _():
                    self.arrival(side, step, block).wait_recv()

                    if step < self.reach:
                        @pl.when(self.sends(side, step + 1))
                        def _():
                            self.copy(side, step + 1, block).start()

    def finish(self, source=None):
        for step in range(1, self.reach + 1):
            for block in range(PLANE):
                for side in (0, 1):
                    @pl.when(self.sends(side, step))
                    def _():
                        self.copy(side, step, block, source[block] if source and step == 1 else None).wait_send()


class Swap:
    def __init__(self, src, dst, sems):
        self.src, self.dst, self.sems = src, dst, sems
        self.pln = lax.axis_index("pln")

    def copy(self, offset):
        peer = across(self.pln, offset)
        return remote(self.src(peer), self.dst(self.pln), self.sems.at[0, offset], self.sems.at[1, offset], {"pln": peer})

    def keep(self):
        return pltpu.make_async_copy(self.src(self.pln), self.dst(self.pln), self.sems.at[0, 0])

    def begin(self):
        for offset in (2, 3, 1):
            self.copy(offset).start()
        self.keep().start()

    def arrived(self, offset):
        self.keep().wait() if offset == 0 else self.copy(offset).wait_recv()

    def finish(self):
        for offset in (1, 2, 3):
            self.copy(offset).wait_send()


VEC_ORDER = ("self_query_bias", "self_value_bias", "cross_value_bias", "self_out_bias", "norm_one_gain", "norm_one_shift",
             "cross_query_bias", "cross_out_bias", "norm_two_gain", "norm_two_shift", "expand_bias", "shrink_bias",
             "norm_three_gain", "norm_three_shift")


def pack_vectors(vecs):
    parts = []
    for v in vecs:
        width = min(128, v.shape[0])
        rows = v.reshape(-1, width)
        parts.append(jnp.pad(rows, ((0, 0), (0, 128 - width))))
    pack = jnp.concatenate(parts)
    return jnp.pad(pack, ((0, -pack.shape[0] % 16), (0, 0)))


def vector_row(pack_ref, wa_count, start, length):
    width = min(128, length)
    pieces = []
    for wa in range(wa_count):
        for row in range(length // width):
            pieces.append(pack_ref[wa, start + row : start + row + 1, :width].astype(jnp.float32))
    return jnp.concatenate(pieces, axis=1)


def split_pairs(value, buffer, column):
    for pair in range(PLANE):
        buffer[pair, :, column : column + 128] = value[:, pair * 128 : pair * 128 + 128]


def opening_kernel(grp_count, wa_count, reach, count, vec_at, content_ref, query_ref, encoder_ref, vec_ref, *refs):
    shards = refs[:count]
    fulls = refs[count : 2 * count]
    vec_out, q_out, kv_out, kv2_out = refs[2 * count : 2 * count + 4]
    held, vec_all, kvbuf, kvbuf2, qbuf, row_sems, vec_sems, line_sems, swap_sems, out_sems = refs[2 * count + 4 :]
    grp, pln, wa = lax.axis_index("grp"), lax.axis_index("pln"), lax.axis_index("wa")
    tok = content_ref.shape[0]
    gathers = [Rows(shards[i], held.at[i] if i < 5 else fulls[i], row_sems, i, wa_count) for i in range(count)]
    greet(grp_count, wa_count)
    vec_keep = pltpu.make_async_copy(vec_ref, vec_all.at[wa], vec_sems.at[0, 0])
    vec_keep.start()
    pushes = [remote(vec_ref, vec_all.at[wa], vec_sems.at[0, o], vec_sems.at[1, o], {"wa": lax.rem(wa + o, wa_count)})
              for o in range(1, wa_count)]
    for g in gathers[:2]:
        g.begin()
    for p in pushes:
        p.start()
    for g in gathers[:2]:
        g.pass_on()
    for g in gathers[2:5]:
        g.begin()
    vec_keep.wait()
    for p in pushes:
        p.wait_recv()
    for g in gathers[:2]:
        g.arrived()
    content = content_ref[...]
    split_pairs(matmul(content, held[0]).astype(jnp.bfloat16), kvbuf, 0)
    row = lambda i: vector_row(vec_all, wa_count, *vec_at[i])
    split_pairs((matmul(content, held[1]) + row(1)).astype(jnp.bfloat16), kvbuf, 128)
    line = Line(kv_out, line_sems, grp_count, reach, tok)
    spot = lambda ref: lambda p: ref.at[pl.ds(pl.multiple_of((grp * PLANE + p) * tok, 16), tok)]
    swap = Swap(lambda p: kvbuf.at[p], spot(kv_out), swap_sems.at[0])
    swap.begin()
    line.send(1, pln, kvbuf.at[pln])
    swap.arrived(1)
    line.send(1, across(pln, 1))
    for g in gathers[2:5]:
        g.pass_on()
    for g in gathers[5:]:
        g.begin()
    for offset in (2, 3):
        swap.arrived(offset)
        line.send(1, across(pln, offset))
    for g in gathers[2:5]:
        g.arrived()
    outs = [pltpu.make_async_copy(held.at[i], fulls[i], out_sems.at[i]) for i in range(5)]
    for o in outs:
        o.start()
    vec_save = pltpu.make_async_copy(vec_all, vec_out, out_sems.at[5])
    vec_save.start()
    query = (matmul(query_ref[...], held[2]) + row(0)).astype(jnp.bfloat16)
    query = query * 0.125
    for pair in range(PLANE):
        qbuf[pair] = query[:, pair * 128 : pair * 128 + 128]
    place = lambda p: q_out.at[pl.ds(pl.multiple_of(p * tok, 16), tok)]
    swap_q = Swap(lambda p: qbuf.at[p], place, swap_sems.at[1])
    swap_q.begin()
    encoder = encoder_ref[...]
    split_pairs(matmul(encoder, held[3]).astype(jnp.bfloat16), kvbuf2, 0)
    split_pairs((matmul(encoder, held[4]) + row(2)).astype(jnp.bfloat16), kvbuf2, 128)
    place2 = lambda p: kv2_out.at[pl.ds(pl.multiple_of(p * tok, 16), tok)]
    swap_2 = Swap(lambda p: kvbuf2.at[p], place2, swap_sems.at[2])
    swap_2.begin()
    for step in range(1, reach + 1):
        line.forward(step)
    swap.arrived(0)
    for s in (swap_q, swap_2):
        for offset in range(4):
            s.arrived(offset)
    for g in gathers[5:]:
        g.pass_on()
    for g in gathers[5:]:
        g.arrived()
    for g in gathers:
        g.finish()
    for p in pushes:
        p.wait_send()
    for o in outs:
        o.wait()
    vec_save.wait()
    line.finish()
    for s in (swap, swap_q, swap_2):
        s.finish()


def run_opening(grp_count, wa_count, content, query, encoder, vecs, mats, vec_at):
    tok = content.shape[0]
    reach = min(grp_count - 1, (DOCLEN + PLANE * tok - 2) // (PLANE * tok))
    count = len(mats)
    low = jnp.bfloat16
    shape = lambda *s: jax.ShapeDtypeStruct(s, low)
    out_shape = [shape(m.shape[0] * wa_count, m.shape[1]) for m in mats]
    out_shape += [shape(wa_count, *vecs.shape), shape(PLANE * tok, 128), shape(grp_count * PLANE * tok, 256),
                  shape(PLANE * tok, 256)]
    return pl.pallas_call(
        functools.partial(opening_kernel, grp_count, wa_count, reach, count, vec_at),
        out_shape=tuple(out_shape),
        in_specs=[VMEM] * 4 + [ANY] * count,
        out_specs=tuple([ANY] * len(out_shape)),
        scratch_shapes=[
            pltpu.VMEM((5, 512, 512), low), pltpu.VMEM((wa_count,) + vecs.shape, low), pltpu.VMEM((PLANE, tok, 256), low),
            pltpu.VMEM((PLANE, tok, 256), low), pltpu.VMEM((PLANE, tok, 128), low),
            DMA((5, count, max(1, wa_count - 1))), DMA((2, wa_count)), DMA((2, 2, reach, PLANE)), DMA((3, 2, 4)), DMA((6,))],
        compiler_params=pltpu.CompilerParams(collective_id=1, has_side_effects=True, vmem_limit_bytes=40 << 20),
    )(content, query, encoder, vecs, *mats)


def to_pairs(value):
    return lax.all_to_all(value, "pln", 1, 0, tiled=True)


def to_tokens(value):
    return lax.all_to_all(value, "pln", 0, 1, tiled=True)


def return_pairs(keys, values):
    both = jnp.concatenate([keys, values], axis=1).astype(jnp.bfloat16)
    mine = lax.psum_scatter(both, "grp", scatter_dimension=0, tiled=True).astype(jnp.bfloat16)
    return to_tokens(mine[:, :128]), to_tokens(mine[:, 128:])


def reduce_grads(grads):
    wa = lax.axis_size("wa")
    mats = [g.astype(jnp.bfloat16).reshape(wa, -1, 512) for g in grads if g.ndim == 2]
    vecs = [g.reshape(wa, -1) for g in grads if g.ndim == 1]
    pack = jnp.concatenate(mats, axis=1)
    mine = lax.psum_scatter(pack, "wa", scatter_dimension=0, tiled=False)
    total = lax.psum(mine, ("grp", "pln")).astype(jnp.float32)
    line = lax.psum(jnp.concatenate(vecs, axis=1).astype(jnp.bfloat16), ("grp", "pln", "wa")).astype(jnp.float32)
    line = lax.dynamic_index_in_dim(line, lax.axis_index("wa"), 0, False)
    out, at, vat = [], 0, 0
    for g in grads:
        if g.ndim == 2:
            n = g.size // wa // 512
            out.append(total[at : at + n].reshape(g.shape[0] // wa, g.shape[1]))
            at += n
        else:
            n = g.size // wa
            out.append(line[vat : vat + n])
            vat += n
    return tuple(out)


def shards(
    query_in,
    content_in,
    encoder_in,
    out_grad,
    document_lengths,
    key_ranks,
    query_limits,
    self_query_weight,
    self_query_bias,
    self_key_weight,
    self_value_weight,
    self_value_bias,
    self_out_weight,
    self_out_bias,
    norm_one_gain,
    norm_one_shift,
    cross_query_weight,
    cross_query_bias,
    cross_key_weight,
    cross_value_weight,
    cross_value_bias,
    cross_out_weight,
    cross_out_bias,
    norm_two_gain,
    norm_two_shift,
    expand_weight,
    expand_bias,
    shrink_weight,
    shrink_bias,
    norm_three_gain,
    norm_three_shift,
):
    grp_count = lax.axis_size("grp")
    own = lax.axis_index("grp")[None].astype(jnp.int32)
    lens = document_lengths
    tok = query_in.shape[1]
    rows = tok * PLANE
    row_at = lax.axis_index("grp") * rows
    cross_keys, cross_marks = mark_tables(lens[0], key_ranks[0], query_limits[0], row_at, rows, False)
    self_keys, self_marks = mark_tables(lens[0], key_ranks[0], query_limits[0], row_at, rows, True)
    wa_count = lax.axis_size("wa")
    vectors = (self_query_bias, self_value_bias, cross_value_bias, self_out_bias, norm_one_gain, norm_one_shift,
        cross_query_bias, cross_out_bias, norm_two_gain, norm_two_shift, expand_bias, shrink_bias, norm_three_gain,
        norm_three_shift)
    vec_at, at = [], 0
    for v in vectors:
        vec_at.append((at, v.shape[0]))
        at += v.shape[0] // min(128, v.shape[0])
    vec_at = tuple(vec_at)
    mats = (self_key_weight, self_value_weight, self_query_weight, cross_key_weight, cross_value_weight, self_out_weight,
        cross_query_weight, cross_out_weight, expand_weight, shrink_weight)
    (self_key_matrix, self_value_mat, self_query_mat, cross_key_matrix, cross_value_mat, self_out_mat, cross_query_mat,
        cross_out_mat, expand_mat, shrink_mat, vec_all, pair_one, kv_one, kv_two) = run_opening(
        grp_count, wa_count, content_in[0], query_in[0], encoder_in[0], pack_vectors(vectors), mats, vec_at)
    lines = [jnp.concatenate([vec_all[w, s : s + n // min(n, 128), : min(n, 128)].reshape(-1) for w in range(wa_count)])
        .astype(jnp.float32) for s, n in vec_at]
    (self_query_vec, self_value_vec, cross_value_vec, self_out_vec, gain_one, shift_one, cross_query_vec, cross_out_vec,
        gain_two, shift_two, expand_vec, shrink_vec, gain_three, shift_three) = lines
    source = query_in[0]
    content_states = content_in[0]
    encoder_output = encoder_in[0]
    cotangent = out_grad[0].astype(jnp.float32)
    kv_two = lax.all_gather(kv_two, "grp", axis=0, tiled=True)
    keys_one, values_one = kv_one[:, :128], kv_one[:, 128:]
    keys_two, values_two = kv_two[:, :128], kv_two[:, 128:]
    attended_one, total_one = attend_forward(True, lens, own, pair_one, self_marks, keys_one, values_one, self_keys)
    mixed_one = to_tokens(attended_one.astype(jnp.bfloat16))
    hidden_one, normed_one, inverse_one = norm_forward(
        source.astype(jnp.float32) + matmul(mixed_one, self_out_mat) + self_out_vec, gain_one, shift_one)
    hidden_one_low = hidden_one.astype(jnp.bfloat16)
    query_two = (matmul(hidden_one_low, cross_query_mat) + cross_query_vec).astype(jnp.bfloat16)
    pair_two = to_pairs(query_two * jnp.bfloat16(0.125))
    attended_two, total_two = attend_forward(False, lens, own, pair_two, cross_marks, keys_two, values_two, cross_keys)
    mixed_two = to_tokens(attended_two.astype(jnp.bfloat16))
    hidden_two, normed_two, inverse_two = norm_forward(
        hidden_one + matmul(mixed_two, cross_out_mat) + cross_out_vec, gain_two, shift_two)
    hidden_two_low = hidden_two.astype(jnp.bfloat16)
    expanded = matmul(hidden_two_low, expand_mat) + expand_vec
    activated = jax.nn.gelu(expanded, approximate=False).astype(jnp.bfloat16)
    layer_out, normed_three, inverse_three = norm_forward(
        hidden_two + matmul(activated, shrink_mat) + shrink_vec, gain_three, shift_three)
    back_three, grad_gain_three, grad_shift_three = norm_backward(cotangent, normed_three, inverse_three, gain_three)
    shrink_in_grad = back_three.astype(jnp.bfloat16)
    grad_shrink_mat = left_product(activated, shrink_in_grad)
    grad_shrink_vec = column_sum(shrink_in_grad)
    activated_grad = right_product(shrink_in_grad, shrink_mat)
    expand_grad = (activated_grad * gelu_slope(expanded)).astype(jnp.bfloat16)
    grad_expand_mat = left_product(hidden_two_low, expand_grad)
    grad_expand_vec = column_sum(expand_grad)
    hidden_two_grad = back_three + right_product(expand_grad, expand_mat)
    back_two, grad_gain_two, grad_shift_two = norm_backward(hidden_two_grad, normed_two, inverse_two, gain_two)
    branch_two = back_two.astype(jnp.bfloat16)
    grad_cross_out_mat = left_product(mixed_two, branch_two)
    grad_cross_out_vec = column_sum(branch_two)
    mixed_two_grad = right_product(branch_two, cross_out_mat).astype(jnp.bfloat16)
    dq_two, dk_two, dv_two = attend_backward(False, lens, own, pair_two, cross_marks, keys_two, values_two, cross_keys,
        attended_two, total_two, to_pairs(mixed_two_grad))
    key_two_low, value_two_low = return_pairs(dk_two, dv_two)
    query_two_low = to_tokens(dq_two)
    grad_cross_query_mat = left_product(hidden_one_low, query_two_low)
    grad_cross_query_vec = column_sum(query_two_low)
    grad_cross_key_mat = left_product(encoder_output, key_two_low)
    grad_cross_value_mat = left_product(encoder_output, value_two_low)
    grad_cross_value_vec = column_sum(value_two_low)
    encoder_grad = right_product(key_two_low, cross_key_matrix) + right_product(value_two_low, cross_value_mat)
    hidden_one_grad = back_two + right_product(query_two_low, cross_query_mat)
    back_one, grad_gain_one, grad_shift_one = norm_backward(hidden_one_grad, normed_one, inverse_one, gain_one)
    branch_one = back_one.astype(jnp.bfloat16)
    grad_self_out_mat = left_product(mixed_one, branch_one)
    grad_self_out_vec = column_sum(branch_one)
    mixed_one_grad = right_product(branch_one, self_out_mat).astype(jnp.bfloat16)
    dq_one, dk_one, dv_one = attend_backward(True, lens, own, pair_one, self_marks, keys_one, values_one, self_keys,
        attended_one, total_one, to_pairs(mixed_one_grad))
    key_one_low, value_one_low = return_pairs(dk_one, dv_one)
    query_one_low = to_tokens(dq_one)
    grad_self_query_mat = left_product(source, query_one_low)
    grad_self_query_vec = column_sum(query_one_low)
    grad_self_key_mat = left_product(content_states, key_one_low)
    grad_self_value_mat = left_product(content_states, value_one_low)
    grad_self_value_vec = column_sum(value_one_low)
    query_grad = back_one + right_product(query_one_low, self_query_mat)
    content_grad = right_product(key_one_low, self_key_matrix) + right_product(value_one_low, self_value_mat)
    grads = reduce_grads((
        grad_self_query_mat, grad_self_query_vec, grad_self_key_mat, grad_self_value_mat, grad_self_value_vec, grad_self_out_mat, grad_self_out_vec, grad_gain_one, grad_shift_one, grad_cross_query_mat, grad_cross_query_vec, grad_cross_key_mat, grad_cross_value_mat, grad_cross_value_vec, grad_cross_out_mat, grad_cross_out_vec, grad_gain_two, grad_shift_two, grad_expand_mat, grad_expand_vec, grad_shrink_mat, grad_shrink_vec, grad_gain_three, grad_shift_three))
    return (layer_out[None], query_grad[None], content_grad[None], encoder_grad[None]) + grads


def solution(mesh):
    ctx, wa = mesh.devices.shape
    mesh = Mesh(mesh.devices.reshape(ctx // PLANE, PLANE, wa), ("grp", "pln", "wa"))
    in_specs = (
        P("wa", ("grp", "pln"), None),
        P("wa", ("grp", "pln"), None),
        P("wa", ("grp", "pln"), None),
        P("wa", ("grp", "pln"), None),
        P("wa", None),
        P("wa", None),
        P("wa", None),
        P("wa", None),
        P("wa"),
        P("wa", None),
        P("wa", None),
        P("wa"),
        P("wa", None),
        P("wa"),
        P("wa"),
        P("wa"),
        P("wa", None),
        P("wa"),
        P("wa", None),
        P("wa", None),
        P("wa"),
        P("wa", None),
        P("wa"),
        P("wa"),
        P("wa"),
        P("wa", None),
        P("wa"),
        P("wa", None),
        P("wa"),
        P("wa"),
        P("wa"),
    )
    out_specs = (
        P("wa", ("grp", "pln"), None),
        P("wa", ("grp", "pln"), None),
        P("wa", ("grp", "pln"), None),
        P("wa", ("grp", "pln"), None),
        P("wa", None),
        P("wa"),
        P("wa", None),
        P("wa", None),
        P("wa"),
        P("wa", None),
        P("wa"),
        P("wa"),
        P("wa"),
        P("wa", None),
        P("wa"),
        P("wa", None),
        P("wa", None),
        P("wa"),
        P("wa", None),
        P("wa"),
        P("wa"),
        P("wa"),
        P("wa", None),
        P("wa"),
        P("wa", None),
        P("wa"),
        P("wa"),
        P("wa"),
    )
    return jax.shard_map(shards, mesh=mesh, in_specs=in_specs, out_specs=out_specs, check_vma=False)
```

profile of v0, /device:TPU:0, one launch (start us, length us, event | category | flops | bytes accessed | tf_op | source)
XLA Modules:
  0.0 603.2 jit_solution(12269328289834099171)
XLA Ops:
  7.3 4.3 concatenate.155
  24.5 55.3 %shard_map.510 = (bf16[512,512]{1,0:T(8,128)(2,1)S(1)}, bf16[512,512]{1,0:T(8,128)(2,1)S(1)}, bf16[512,512]{1,0:T(8,128)(2,1)S(1)}, bf16[512,512]{1,0:T(8,128)(2...) custom-call(bf16[256,512]{1,0:T(8,128)(2,1)S(1)} %bitcast.226, ...), custom_call_target="tpu_custom_call" | custom-call | tf_op jit(solution)/shard_map/pallas_call | solution.py:576
  87.5 3.0 fusion.71
  90.5 2.0 fusion.48
  92.6 2.8 fusion.3
  95.4 1.6 pad_maximum_fusion.2.km_ref
  99.7 9.6 %shard_map.511 = (f32[1024,128]{1,0:T(8,128)}, f32[1024,128]{1,0:T(8,128)}) custom-call(s32[1,4]{1,0:T(1,128)} %lens_ref.7, s32[1]{0:T(128)} %bitcast.1.own_ref, bf16[1024,128]{1,0:T(8,128)(2,1)} %copy-done.8, bf16[1024,128]{1,0:T(8,128)(2,1)} %pad_maximum_fusion.4.qm_ref, bf16[4096,128]{1,0:T(8,128)(2,1)} %get-tuple-element.106.k_ref, ...), custom_call_target="tpu_custom_call" | custom-call | tf_op jit(solution)/shard_map/pallas_call | solution.py:117
  109.4 1.8 convert_element_type.231
  111.1 1.8 copy.62
  113.0 4.1 all-to-all-start
  119.1 3.3 pad_maximum_fusion.3.km_ref
  126.1 4.0 all-to-all-start.1
  131.2 3.0 fusion.70
  134.2 2.1 all-to-all-done.1
  136.2 10.2 %shard_map.512 = (f32[1024,128]{1,0:T(8,128)}, f32[1024,128]{1,0:T(8,128)}) custom-call(s32[1,4]{1,0:T(1,128)} %lens_ref.7, s32[1]{0:T(128)} %bitcast.1.own_ref, bf16[1024,128]{1,0:T(8,128)(2,1)} %bitcast.35.q_ref, bf16[1024,128]{1,0:T(8,128)(2,1)} %pad_maximum_fusion.5.qm_ref, bf16[4096,128]{1,0:T(8,128)(2,1)} %get-tuple-element.104.k_ref, ...), custom_call_target="tpu_custom_call" | custom-call | tf_op jit(solution)/shard_map/pallas_call | solution.py:117
  146.4 1.8 convert_element_type.238
  148.2 1.8 copy.64
  150.0 4.0 all-to-all-start.2
  154.3 5.8 all-to-all-done.2
  160.2 1.7 fusion.76
  162.1 5.1 fusion.6
  173.2 9.1 %all_to_all.209 = bf16[256,4,128]{2,0,1:T(8,128)(2,1)} all-to-all(bf16[256,4,128]{2,0,1:T(8,128)(2,1)S(1)} %bitcast.248), channel_id=1, replica_groups=mesh['grp'=4,'pln'=4,'wa'=2] {'pln'}, dimensions={1} | all-to-all | bytes 524288 | tf_op jit(solution)/shard_map/all_to_all | solution.py:590
  182.3 16.4 %shard_map.513 = (bf16[1024,128]{1,0:T(8,128)(2,1)}, f32[4096,128]{1,0:T(8,128)}, f32[4096,128]{1,0:T(8,128)}) custom-call(s32[1,4]{1,0:T(1,128)} %lens_ref.7, s32[1]{0:T(128)} %bitcast.1.own_ref, bf16[1024,128]{1,0:T(8,128)(2,1)} %bitcast.35.q_ref, bf16[1024,128]{1,0:T(8,128)(2,1)} %pad_maximum_fusion.5.qm_ref, bf16[4096,128]{1,0:T(8,128)(2,1)} %get-tuple-element.104.k_ref, ...), custom_call_target="tpu_custom_call" | custom-call | tf_op jit(solution)/shard_map/pallas_call | solution.py:200
  198.7 1.8 convert.91
  201.0 1.6 pad_maximum_fusion.1
  202.7 1.8 copy.66
  204.5 9.5 %all_to_all.210 = bf16[4,256,128]{1,2,0:T(8,128)(2,1)S(1)} all-to-all(bf16[4,256,128]{1,2,0:T(8,128)(2,1)} %copy.66), channel_id=1, replica_groups=mesh['grp'=4,'pln'=4,'wa'=2] {'pln'}, dimensions={0} | all-to-all | bytes 524288 | tf_op jit(solution)/shard_map/all_to_all | solution.py:594
  214.0 1.8 multiply_reduce_fusion.1
  216.6 9.1 %all_to_all.211 = bf16[256,4,128]{2,0,1:T(8,128)(2,1)} all-to-all(bf16[256,4,128]{2,0,1:T(8,128)(2,1)S(1)} %bitcast.249), channel_id=1, replica_groups=mesh['grp'=4,'pln'=4,'wa'=2] {'pln'}, dimensions={1} | all-to-all | bytes 524288 | tf_op jit(solution)/shard_map/all_to_all | solution.py:590
  225.6 16.2 %shard_map.514 = (bf16[1024,128]{1,0:T(8,128)(2,1)}, f32[4096,128]{1,0:T(8,128)}, f32[4096,128]{1,0:T(8,128)}) custom-call(s32[1,4]{1,0:T(1,128)} %lens_ref.7, s32[1]{0:T(128)} %bitcast.1.own_ref, bf16[1024,128]{1,0:T(8,128)(2,1)} %copy-done.8, bf16[1024,128]{1,0:T(8,128)(2,1)} %pad_maximum_fusion.4.qm_ref, bf16[4096,128]{1,0:T(8,128)(2,1)} %get-tuple-element.106.k_ref, ...), custom_call_target="tpu_custom_call" | custom-call | tf_op jit(solution)/shard_map/pallas_call | solution.py:200
  241.9 1.8 convert.89
  244.2 1.5 pad_maximum_fusion
  246.8 3.4 convolution_convert_fusion.1
  250.2 4.5 reshape.532
  254.7 2.0 convolution_convert_fusion.2
  256.7 3.5 convolution_convert_fusion
  260.2 2.0 convolution_convert_fusion.6
  263.5 1.8 copy.68
  265.3 3.4 all-to-all-start.6
  268.8 7.6 %reduce-scatter.6.cloned.1.call-done = bf16[1024,256]{1,0:T(8,128)(2,1)} async-done(((bf16[4096,256]{1,0:T(8,128)(2,1)}), bf16[1024,256]{1,0:T(8,128)(2,1)}) %reduce-scatter.6.cloned.1.call-update) | async-done | bytes 524304 | tf_op jit(solution)/shard_map/reduce_scatter | solution.py:599
  276.3 1.9 fusion.72
  278.2 1.8 copy.71
  280.0 4.1 all-to-all-start.9
  285.2 1.8 copy.72
  287.0 3.1 all-to-all-done.9
  290.2 3.4 all-to-all-start.10
  293.6 2.1 convolution_convert_fusion.4
  295.7 41.1 %reduce-scatter.4.cloned.1.call-done = bf16[1024,256]{1,0:T(8,128)(2,1)} async-done(((bf16[4096,256]{1,0:T(8,128)(2,1)}), bf16[1024,256]{1,0:T(8,128)(2,1)}) %reduce-scatter.4.cloned.1.call-update) | async-done | bytes 524304 | tf_op jit(solution)/shard_map/reduce_scatter | solution.py:599
  336.8 1.9 fusion.73
  338.7 1.8 copy.69
  340.5 4.1 all-to-all-start.7
  345.7 1.8 copy.70
  347.5 3.2 all-to-all-done.7
  350.6 3.4 all-to-all-start.8
  354.1 2.1 convolution_convert_fusion.8
  356.2 3.9 all-to-all-done.8
  360.4 1.9 constant_dynamic-update-slice_fusion.8
  373.9 2.1 fusion.23
  378.9 92.7 %reduce-scatter.8.cloned.1.call-done = bf16[1,4096,512]{2,1,0:T(8,128)(2,1)} async-done(((bf16[2,4096,512]{2,1,0:T(8,128)(2,1)}), bf16[1,4096,512]{2,1,0:T(8,128)(2,1)}) %reduce-scatter.8.cloned.1.call-update) | async-done | bytes 4194320 | tf_op jit(solution)/shard_map/reduce_scatter | solution.py:608
  471.7 41.1 %psum.15 = bf16[2,4352]{1,0:T(2,128)(2,1)S(1)} all-reduce(bf16[2,4352]{1,0:T(2,128)(2,1)S(1)} %constant_dynamic-update-slice_fusion.10), channel_id=1, replica_groups=mesh['grp'=4,'pln'=4,'wa'=2] {'grp','pln','wa'}, use_global_device_ids=true, to_apply=%region_33.34 | all-reduce | flops 8704 | bytes 34816 | tf_op jit(solution)/shard_map/psum | solution.py:610
  516.5 71.2 %all-reduce.3.cloned.1.call-done = bf16[4096,512]{1,0:T(8,128)(2,1)} async-done(((bf16[4096,512]{1,0:T(8,128)(2,1)}), bf16[4096,512]{1,0:T(8,128)(2,1)}) %all-reduce.3.cloned.1.call-update) | async-done | bytes 4194320 | tf_op jit(solution)/shard_map/psum | solution.py:609
  587.7 3.5 fusion.68
  591.2 1.9 reshape.548
  593.1 3.6 fusion.69
  (235 shorter events, 61.3 us)
Async XLA Ops:
  7.2 124.0 %all-gather.2.cloned.1.call-start = ((), (), s32[]{:S(2)}) async-start(), calls=%async_computation.14 | async-start | bytes 2621440 | tf_op jit(solution)/shard_map/all_gather | solution.py:688
  11.6 0.9 copy-start
  12.5 0.9 copy-start.2
  13.5 0.9 copy-start.4
  14.4 1.2 copy-start.6
  15.6 1.2 copy-start.7
  16.9 0.9 copy-start.15
  17.8 0.9 copy-start.16
  18.8 0.9 copy-start.17
  19.7 0.9 copy-start.18
  20.7 0.9 copy-start.19
  21.6 0.9 copy-start.20
  22.6 0.9 copy-start.21
  23.5 0.9 copy-start.22
  24.5 61.1 %copy-start.56 = (s32[1,4]{1,0:T(1,128)S(1)}, s32[1,4]{1,0:T(1,128)}, u32[]{:S(2)}) copy-start(s32[1,4]{1,0:T(1,128)} %lens_ref.7) | copy-start | bytes 52
  82.9 1.3 copy-start.23
  84.2 1.3 copy-start.25
  87.5 3.1 copy-start.55
  111.1 12.0 %copy-start.1 = (bf16[1,256,512]{2,1,0:T(8,128)(2,1)S(1)}, bf16[1,256,512]{2,1,0:T(8,128)(2,1)}, u32[]{:S(2)}) copy-start(bf16[1,256,512]{2,1,0:T(8,128)(2,1)} %param.31) | copy-start | bytes 786436
  113.0 10.2 %all-to-all-start = ((bf16[4,256,128]{1,2,0:T(8,128)(2,1)}), bf16[4,256,128]{1,2,0:T(8,128)(2,1)}, u32[]{:S(2)}, u32[]{:S(2)}) async-start(bf16[4,256,128]{1,2,0:T(8,128)(2,1)} %copy.62), calls=%async_computation | async-start | bytes 524288 | tf_op jit(solution)/shard_map/all_to_all | solution.py:594
  123.1 1.7 copy-start.13
  126.1 10.2 %all-to-all-start.1 = ((bf16[256,4,128]{2,0,1:T(8,128)(2,1)}), bf16[256,4,128]{2,0,1:T(8,128)(2,1)}, u32[]{:S(2)}, u32[]{:S(2)}) async-start(bf16[256,4,128]{2,0,1:T(8,128)(2,1)} %bitcast.247), calls=%async_computation.1 | async-start | bytes 524288 | tf_op jit(solution)/shard_map/all_to_all | solution.py:590
  150.0 10.1 %all-to-all-start.2 = ((bf16[4,256,128]{1,2,0:T(8,128)(2,1)}), bf16[4,256,128]{1,2,0:T(8,128)(2,1)}, u32[]{:S(2)}, u32[]{:S(2)}) async-start(bf16[4,256,128]{1,2,0:T(8,128)(2,1)} %copy.64), calls=%async_computation.2 | async-start | bytes 524288 | tf_op jit(solution)/shard_map/all_to_all | solution.py:594
  154.1 122.3 %reduce-scatter.6.cloned.1.call-start = ((), (), s32[]{:S(2)}) async-start(), calls=%async_computation.16 | async-start | bytes 2621440 | tf_op jit(solution)/shard_map/reduce_scatter | solution.py:599
  160.2 1.9 copy-start.24
  161.8 10.3 %copy-start.32 = (f32[256,512]{1,0:T(8,128)}, f32[256,512]{1,0:T(8,128)S(1)}, u32[]{:S(2)}) copy-start(f32[256,512]{1,0:T(8,128)S(1)} %get-tuple-element.152) | copy-start | bytes 1572868
  162.1 5.1 copy-start.26
  167.2 1.0 copy-start.53
  167.2 1.2 copy-start.44
  169.7 1.4 copy-start.45
  171.1 1.0 copy-start.54
  198.7 2.2 copy-start.48
  202.6 11.5 %copy-start.14 = (bf16[512,512]{1,0:T(8,128)(2,1)S(1)}, bf16[512,512]{1,0:T(8,128)(2,1)}, u32[]{:S(2)}) copy-start(bf16[512,512]{1,0:T(8,128)(2,1)} %copy-done.12) | copy-start | bytes 1572868
  202.6 134.2 %reduce-scatter.4.cloned.1.call-start = ((), (), s32[]{:S(2)}) async-start(), calls=%async_computation.15 | async-start | bytes 2621440 | tf_op jit(solution)/shard_map/reduce_scatter | solution.py:599
  204.5 11.4 %copy-start.28 = (f32[256,512]{1,0:T(8,128)S(1)}, f32[256,512]{1,0:T(8,128)}, u32[]{:S(2)}) copy-start(f32[256,512]{1,0:T(8,128)} %copy-done.27) | copy-start | bytes 1572868
  214.0 2.5 copy-start.36
  241.9 2.2 copy-start.47
  245.8 1.0 copy-start.33
  250.2 4.5 copy-start.35
  256.7 5.5 copy-start.29
  256.7 5.5 copy-start.37
  265.3 14.7 %all-to-all-start.6 = ((bf16[4,256,128]{1,2,0:T(8,128)(2,1)}), bf16[4,256,128]{1,2,0:T(8,128)(2,1)S(1)}, u32[]{:S(2)}, u32[]{:S(2)}) async-start(bf16[4,256,128]{1,2,0:T(8,128)(2,1)} %copy.68), calls=%async_computation.6 | async-start | bytes 524288 | tf_op jit(solution)/shard_map/all_to_all | solution.py:594
  278.2 15.4 %copy-start.3 = (bf16[1,256,512]{2,1,0:T(8,128)(2,1)S(1)}, bf16[1,256,512]{2,1,0:T(8,128)(2,1)}, u32[]{:S(2)}) copy-start(bf16[1,256,512]{2,1,0:T(8,128)(2,1)} %param.33) | copy-start | bytes 786436
  280.0 13.6 %copy-start.41 = (bf16[4,256,128]{1,2,0:T(8,128)(2,1)}, bf16[4,256,128]{1,2,0:T(8,128)(2,1)S(1)}, u32[]{:S(2)}) copy-start(bf16[4,256,128]{1,2,0:T(8,128)(2,1)S(1)} %all-to-all-done.6) | copy-start | bytes 786436
  280.0 10.2 %all-to-all-start.9 = ((bf16[4,256,128]{1,2,0:T(8,128)(2,1)}), bf16[4,256,128]{1,2,0:T(8,128)(2,1)}, u32[]{:S(2)}, u32[]{:S(2)}) async-start(bf16[4,256,128]{1,2,0:T(8,128)(2,1)} %copy.71), calls=%async_computation.11 | async-start | bytes 524288 | tf_op jit(solution)/shard_map/all_to_all | solution.py:594
  290.2 50.3 %all-to-all-start.10 = ((bf16[4,256,128]{1,2,0:T(8,128)(2,1)}), bf16[4,256,128]{1,2,0:T(8,128)(2,1)S(1)}, u32[]{:S(2)}, u32[]{:S(2)}) async-start(bf16[4,256,128]{1,2,0:T(8,128)(2,1)} %copy.72), calls=%async_computation.12 | async-start | bytes 524288 | tf_op jit(solution)/shard_map/all_to_all | solution.py:594
  295.7 58.4 %copy-start.5 = (bf16[1,256,512]{2,1,0:T(8,128)(2,1)S(1)}, bf16[1,256,512]{2,1,0:T(8,128)(2,1)}, u32[]{:S(2)}) copy-start(bf16[1,256,512]{2,1,0:T(8,128)(2,1)} %param.32) | copy-start | bytes 786436
  340.5 19.9 %copy-start.42 = (bf16[4,256,128]{1,2,0:T(8,128)(2,1)}, bf16[4,256,128]{1,2,0:T(8,128)(2,1)S(1)}, u32[]{:S(2)}) copy-start(bf16[4,256,128]{1,2,0:T(8,128)(2,1)S(1)} %all-to-all-done.10) | copy-start | bytes 786436
  340.5 10.2 %all-to-all-start.7 = ((bf16[4,256,128]{1,2,0:T(8,128)(2,1)}), bf16[4,256,128]{1,2,0:T(8,128)(2,1)}, u32[]{:S(2)}, u32[]{:S(2)}) async-start(bf16[4,256,128]{1,2,0:T(8,128)(2,1)} %copy.69), calls=%async_computation.8 | async-start | bytes 524288 | tf_op jit(solution)/shard_map/all_to_all | solution.py:594
  350.6 9.4 %all-to-all-start.8 = ((bf16[4,256,128]{1,2,0:T(8,128)(2,1)}), bf16[4,256,128]{1,2,0:T(8,128)(2,1)S(1)}, u32[]{:S(2)}, u32[]{:S(2)}) async-start(bf16[4,256,128]{1,2,0:T(8,128)(2,1)} %copy.70), calls=%async_computation.9 | async-start | bytes 524288 | tf_op jit(solution)/shard_map/all_to_all | solution.py:594
  354.0 117.5 %reduce-scatter.8.cloned.1.call-start = ((), (), s32[]{:S(2)}) async-start(), calls=%async_computation.17 | async-start | bytes 12582912 | tf_op jit(solution)/shard_map/reduce_scatter | solution.py:608
  360.0 4.0 copy-start.39
  360.0 3.1 copy-start.50
  360.1 4.0 copy-start.46
  360.4 4.5 copy-start.51
  362.3 3.4 copy-start.52
  363.2 3.4 copy-start.49
  364.0 3.4 copy-start.31
  367.4 2.3 copy-start.30
  371.2 1.3 copy-start.38
  371.3 4.9 copy-start.10
  371.3 216.5 %all-reduce.3.cloned.1.call-start = ((), (), s32[]{:S(2)}) async-start(), calls=%async_computation.18 | async-start | bytes 8388608 | tf_op jit(solution)/shard_map/psum | solution.py:609
  372.7 3.3 copy-start.43
  376.0 2.6 copy-start.40
  (6 other events, 4.7 us)
Sparse Core Ops, SparseCore 0:
  85.7 45.4 all-gather.1
  202.7 73.5 reduce-scatter.5
  279.3 57.4 reduce-scatter.3
  371.4 100.1 reduce-scatter.7
  475.5 112.1 all-reduce.2
where the time goes:
time: 597 us; the launch traced here: 603 us
  waiting for transfers between devices  233 us (39%)
  Pallas kernels  108 us (18%)
  local copies, waits for them, and re-layouts  79.1 us (13%)
  blocking collectives  68.9 us (12%)
  matrix products  39.4 us (7%)
  starting transfers between devices  30.9 us (5%)
  other arithmetic  30.2 us (5%)
  between operations  14.5 us (2%)
    reduce_scatter x1, waiting for transfers between devices, reduce_grads(): mine = lax.psum_scatter(pack, 'wa', scatter_dimension=0, tiled=False)  92.7 us
    psum x1, waiting for transfers between devices, reduce_grads(): total = lax.psum(mine, ('grp', 'pln')).astype(jnp.float32)  71.2 us
    pallas_call x1, Pallas kernels, run_opening(): pl.pallas_call(functools.partial(opening_kernel, grp_count, wa_count, rea...  55.3 us
    reduce_scatter x2, waiting for transfers between devices, return_pairs(): lax.psum_scatter(both, 'grp', scatter_dimension=0, tiled=True)  48.7 us
    psum x1, blocking collectives, reduce_grads(): lax.psum(jnp.concatenate(vecs, axis=1).astype(jnp.bfloat16), ('grp', 'pln...  41.1 us
    pallas_call x2, Pallas kernels, attend_backward(): pl.pallas_call(functools.partial(backward_kernel, ranked), out_shape=(jax...  32.6 us
    unnamed x136, local copies, waits for them, and re-layouts  31.6 us
    all_to_all x7, starting transfers between devices, to_tokens(): return lax.all_to_all(value, 'pln', 0, 1, tiled=True)  26.4 us
  transfers between devices with their start and end apart: 13, of which 11 were waited for; matrix products, arithmetic and copies ran while one was open for 14% of the time, Pallas kernels for 4%

commit v1 on v0

--- a/solution.py
+++ b/solution.py
@@ -119,7 +119,7 @@
         out_shape=(jax.ShapeDtypeStruct((rows, 128), jnp.float32),) * 2,
         in_specs=[smem, smem] + [whole] * 5,
         out_specs=(whole, whole),
-        compiler_params=pltpu.CompilerParams(vmem_limit_bytes=56 << 20),
+        compiler_params=pltpu.CompilerParams(vmem_limit_bytes=60 << 20),
     )(lens, own, q, qm, k, v, km)
 
 
@@ -202,7 +202,7 @@
         out_shape=(jax.ShapeDtypeStruct((rows, 128), jnp.bfloat16),) + (jax.ShapeDtypeStruct((keys, 128), jnp.float32),) * 2,
         in_specs=[smem, smem] + [whole] * 8,
         out_specs=(whole, whole, whole),
-        compiler_params=pltpu.CompilerParams(vmem_limit_bytes=56 << 20),
+        compiler_params=pltpu.CompilerParams(vmem_limit_bytes=60 << 20),
     )(lens, own, q, qm, k, v, km, o, lse, do)
 
 
@@ -582,8 +582,118 @@
             pltpu.VMEM((5, 512, 512), low), pltpu.VMEM((wa_count,) + vecs.shape, low), pltpu.VMEM((PLANE, tok, 256), low),
             pltpu.VMEM((PLANE, tok, 256), low), pltpu.VMEM((PLANE, tok, 128), low),
             DMA((5, count, max(1, wa_count - 1))), DMA((2, wa_count)), DMA((2, 2, reach, PLANE)), DMA((3, 2, 4)), DMA((6,))],
-        compiler_params=pltpu.CompilerParams(collective_id=1, has_side_effects=True, vmem_limit_bytes=40 << 20),
+        compiler_params=pltpu.CompilerParams(collective_id=1, has_side_effects=True, vmem_limit_bytes=60 << 20),
     )(content, query, encoder, vecs, *mats)
+
+
+def flat_pairs(buffer):
+    return jnp.concatenate([buffer[p] for p in range(PLANE)], axis=1)
+
+
+def middle_kernel(grp_count, wa_count, reach, vec_at, attended_ref, query_ref, out_mat_ref, query_mat_ref, vec_ref,
+                  kv_own_ref, expand_ref, shrink_ref,
+                  hidden_ref, normed_ref, inverse_ref, mixed_ref, q_out, kv_out, expand_full, shrink_full,
+                  sendbuf, mixbuf, qbuf, row_sems, line_sems, swap_sems, keep_sem):
+    grp, pln = lax.axis_index("grp"), lax.axis_index("pln")
+    tok = query_ref.shape[0]
+    gathers = [Rows(expand_ref, expand_full, row_sems, 0, wa_count), Rows(shrink_ref, shrink_full, row_sems, 1, wa_count)]
+    for p in range(PLANE):
+        sendbuf[p] = attended_ref[p * tok : p * tok + tok, :].astype(jnp.bfloat16)
+    greet(grp_count, wa_count)
+    swap = Swap(lambda p: sendbuf.at[p], lambda p: mixbuf.at[p], swap_sems.at[0])
+    swap.begin()
+    line = Line(kv_out, line_sems, grp_count, reach, tok)
+    sources = [kv_own_ref.at[pl.ds(b * tok, tok)] for b in range(PLANE)]
+    for b in range(PLANE):
+        line.send(1, b, sources[b])
+    for g in gathers:
+        g.begin()
+    whole = pl.ds(pl.multiple_of(grp * PLANE * tok, 16), PLANE * tok)
+    keep = pltpu.make_async_copy(kv_own_ref, kv_out.at[whole], keep_sem)
+    keep.start()
+    row = lambda i: vector_row(vec_ref, wa_count, *vec_at[i])
+    for offset in range(4):
+        swap.arrived(offset)
+    mixed = flat_pairs(mixbuf)
+    mixed_ref[...] = mixed
+    value = query_ref[...].astype(jnp.float32) + matmul(mixed, out_mat_ref[...]) + row(3)
+    hidden, normed, inverse = norm_forward(value, row(4), row(5))
+    hidden_ref[...] = hidden
+    normed_ref[...] = normed
+    inverse_ref[...] = jnp.broadcast_to(inverse, inverse_ref.shape)
+    query = (matmul(hidden.astype(jnp.bfloat16), query_mat_ref[...]) + row(6)).astype(jnp.bfloat16) * 0.125
+    for pair in range(PLANE):
+        qbuf[pair] = query[:, pair * 128 : pair * 128 + 128]
+    place = lambda p: q_out.at[pl.ds(pl.multiple_of(p * tok, 16), tok)]
+    swap_q = Swap(lambda p: qbuf.at[p], place, swap_sems.at[1])
+    swap_q.begin()
+    line.forward(1)
+    for g in gathers:
+        g.pass_on()
+    for step in range(2, reach + 1):
+        line.forward(step)
+    for offset in range(4):
+        swap_q.arrived(offset)
+    for g in gathers:
+        g.arrived()
+    for g in gathers:
+        g.finish()
+    line.finish(sources)
+    keep.wait()
+    swap.finish()
+    swap_q.finish()
+
+
+def run_middle(grp_count, wa_count, attended, query, out_mat, query_mat, vecs, vec_at, kv_own, expand, shrink):
+    tok = query.shape[0]
+    reach = min(grp_count - 1, (DOCLEN + PLANE * tok - 2) // (PLANE * tok))
+    low, full = jnp.bfloat16, jnp.float32
+    shape = jax.ShapeDtypeStruct
+    return pl.pallas_call(
+        functools.partial(middle_kernel, grp_count, wa_count, reach, vec_at),
+        out_shape=(shape((tok, 512), full), shape((tok, 512), full), shape((tok, 128), full), shape((tok, 512), low),
+                   shape((PLANE * tok, 128), low), shape((grp_count * PLANE * tok, 256), low),
+                   shape((expand.shape[0] * wa_count, expand.shape[1]), low),
+                   shape((shrink.shape[0] * wa_count, shrink.shape[1]), low)),
+        in_specs=[VMEM] * 5 + [ANY] * 3,
+        out_specs=tuple([VMEM] * 4 + [ANY] * 4),
+        scratch_shapes=[
+            pltpu.VMEM((PLANE, tok, 128), low), pltpu.VMEM((PLANE, tok, 128), low), pltpu.VMEM((PLANE, tok, 128), low),
+            DMA((5, 2, max(1, wa_count - 1))), DMA((2, 2, reach, PLANE)), DMA((2, 2, 4)), DMA],
+        compiler_params=pltpu.CompilerParams(collective_id=2, has_side_effects=True, vmem_limit_bytes=60 << 20),
+    )(attended, query, out_mat, query_mat, vecs, kv_own, expand, shrink)
+
+
+def swap_kernel(inverse, in_ref, out_ref, sendbuf, getbuf, swap_sems):
+    tok = getbuf.shape[1]
+    for p in range(PLANE):
+        if inverse:
+            sendbuf[p] = in_ref[p * tok : p * tok + tok, :].astype(jnp.bfloat16)
+        else:
+            sendbuf[p] = in_ref[:, p * 128 : p * 128 + 128].astype(jnp.bfloat16)
+    greet(1, 1, groups=False, rows=False)
+    swap = Swap(lambda p: sendbuf.at[p], lambda p: getbuf.at[p], swap_sems)
+    swap.begin()
+    for offset in range(4):
+        swap.arrived(offset)
+    for p in range(PLANE):
+        if inverse:
+            out_ref[:, p * 128 : p * 128 + 128] = getbuf[p]
+        else:
+            out_ref[p * tok : p * tok + tok, :] = getbuf[p]
+    swap.finish()
+
+
+def run_swap(inverse, value, ident):
+    tok = value.shape[0] // PLANE if inverse else value.shape[0]
+    low = jnp.bfloat16
+    return pl.pallas_call(
+        functools.partial(swap_kernel, inverse),
+        out_shape=jax.ShapeDtypeStruct((tok, 512) if inverse else (PLANE * tok, 128), low),
+        in_specs=[VMEM], out_specs=VMEM,
+        scratch_shapes=[pltpu.VMEM((PLANE, tok, 128), low), pltpu.VMEM((PLANE, tok, 128), low), DMA((2, 4))],
+        compiler_params=pltpu.CompilerParams(collective_id=ident, has_side_effects=True, vmem_limit_bytes=60 << 20),
+    )(value)
 
 
 def to_pairs(value):
@@ -673,9 +783,9 @@
         at += v.shape[0] // min(128, v.shape[0])
     vec_at = tuple(vec_at)
     mats = (self_key_weight, self_value_weight, self_query_weight, cross_key_weight, cross_value_weight, self_out_weight,
-        cross_query_weight, cross_out_weight, expand_weight, shrink_weight)
+        cross_query_weight, cross_out_weight)
     (self_key_matrix, self_value_mat, self_query_mat, cross_key_matrix, cross_value_mat, self_out_mat, cross_query_mat,
-        cross_out_mat, expand_mat, shrink_mat, vec_all, pair_one, kv_one, kv_two) = run_opening(
+        cross_out_mat, vec_all, pair_one, kv_one, kv_two_own) = run_opening(
         grp_count, wa_count, content_in[0], query_in[0], encoder_in[0], pack_vectors(vectors), mats, vec_at)
     lines = [jnp.concatenate([vec_all[w, s : s + n // min(n, 128), : min(n, 128)].reshape(-1) for w in range(wa_count)])
         .astype(jnp.float32) for s, n in vec_at]
@@ -685,18 +795,16 @@
     content_states = content_in[0]
     encoder_output = encoder_in[0]
     cotangent = out_grad[0].astype(jnp.float32)
-    kv_two = lax.all_gather(kv_two, "grp", axis=0, tiled=True)
     keys_one, values_one = kv_one[:, :128], kv_one[:, 128:]
+    attended_one, total_one = attend_forward(True, lens, own, pair_one, self_marks, keys_one, values_one, self_keys)
+    hidden_one, normed_one, inverse_one, mixed_one, pair_two, kv_two, expand_mat, shrink_mat = run_middle(
+        grp_count, wa_count, attended_one, source, self_out_mat, cross_query_mat, vec_all, vec_at, kv_two_own,
+        expand_weight, shrink_weight)
+    inverse_one = inverse_one[:, :1]
+    hidden_one_low = hidden_one.astype(jnp.bfloat16)
     keys_two, values_two = kv_two[:, :128], kv_two[:, 128:]
-    attended_one, total_one = attend_forward(True, lens, own, pair_one, self_marks, keys_one, values_one, self_keys)
-    mixed_one = to_tokens(attended_one.astype(jnp.bfloat16))
-    hidden_one, normed_one, inverse_one = norm_forward(
-        source.astype(jnp.float32) + matmul(mixed_one, self_out_mat) + self_out_vec, gain_one, shift_one)
-    hidden_one_low = hidden_one.astype(jnp.bfloat16)
-    query_two = (matmul(hidden_one_low, cross_query_mat) + cross_query_vec).astype(jnp.bfloat16)
-    pair_two = to_pairs(query_two * jnp.bfloat16(0.125))
     attended_two, total_two = attend_forward(False, lens, own, pair_two, cross_marks, keys_two, values_two, cross_keys)
-    mixed_two = to_tokens(attended_two.astype(jnp.bfloat16))
+    mixed_two = run_swap(True, attended_two, 3)
     hidden_two, normed_two, inverse_two = norm_forward(
         hidden_one + matmul(mixed_two, cross_out_mat) + cross_out_vec, gain_two, shift_two)
     hidden_two_low = hidden_two.astype(jnp.bfloat16)
@@ -719,9 +827,9 @@
     grad_cross_out_vec = column_sum(branch_two)
     mixed_two_grad = right_product(branch_two, cross_out_mat).astype(jnp.bfloat16)
     dq_two, dk_two, dv_two = attend_backward(False, lens, own, pair_two, cross_marks, keys_two, values_two, cross_keys,
-        attended_two, total_two, to_pairs(mixed_two_grad))
+        attended_two, total_two, run_swap(False, mixed_two_grad, 4))
     key_two_low, value_two_low = return_pairs(dk_two, dv_two)
-    query_two_low = to_tokens(dq_two)
+    query_two_low = run_swap(True, dq_two, 6)
     grad_cross_query_mat = left_product(hidden_one_low, query_two_low)
     grad_cross_query_vec = column_sum(query_two_low)
     grad_cross_key_mat = left_product(encoder_output, key_two_low)
@@ -735,9 +843,9 @@
     grad_self_out_vec = column_sum(branch_one)
     mixed_one_grad = right_product(branch_one, self_out_mat).astype(jnp.bfloat16)
     dq_one, dk_one, dv_one = attend_backward(True, lens, own, pair_one, self_marks, keys_one, values_one, self_keys,
-        attended_one, total_one, to_pairs(mixed_one_grad))
+        attended_one, total_one, run_swap(False, mixed_one_grad, 5))
     key_one_low, value_one_low = return_pairs(dk_one, dv_one)
-    query_one_low = to_tokens(dq_one)
+    query_one_low = run_swap(True, dq_one, 7)
     grad_self_query_mat = left_product(source, query_one_low)
     grad_self_query_vec = column_sum(query_one_low)
     grad_self_key_mat = left_product(content_states, key_one_low)

time: 597 us -> 669 us (1.12)
  Pallas kernels: 108 us -> 230 us
  waiting for transfers between devices: 233 us -> 276 us
  local copies, waits for them, and re-layouts: 79.1 us -> 44.3 us
  blocking collectives: 68.9 us -> 41.2 us
  starting transfers between devices: 30.9 us -> 14.4 us
  other arithmetic: 30.2 us -> 20.1 us
    pallas_call x0 -> x6, Pallas kernels: none -> 129 us  [the longest x1 92.8 us: run_middle(): pl.pallas_call(functools.partial(middle_kernel, grp_count, wa_count, reac...]
    reduce_scatter x2, waiting for transfers between devices: 48.7 us -> 101 us  [return_pairs(): lax.psum_scatter(both, 'grp', scatter_dimension=0, tiled=True)]
    all_to_all x3 -> x0, blocking collectives: 27.8 us -> none  [the longest x2 18.2 us: to_pairs(): return lax.all_to_all(value, 'pln', 1, 0, tiled=True)]
    unnamed x136 -> x100, local copies, waits for them, and re-layouts: 31.6 us -> 11.1 us
    all_to_all x7 -> x4, starting transfers between devices: 26.4 us -> 14.3 us  [to_tokens(): return lax.all_to_all(value, 'pln', 0, 1, tiled=True)]
    all_to_all x8 -> x4, local copies, waits for them, and re-layouts: 14.5 us -> 4.34 us  [to_tokens(): return lax.all_to_all(value, 'pln', 0, 1, tiled=True)]
    pallas_call x1, Pallas kernels: 55.3 us -> 48 us  [run_opening(): pl.pallas_call(functools.partial(opening_kernel, grp_count, wa_count, rea...]
    all_to_all x7 -> x4, waiting for transfers between devices: 16.8 us -> 11.7 us  [to_tokens(): return lax.all_to_all(value, 'pln', 0, 1, tiled=True)]
  transfers between devices with their start and end apart: 13 -> 8, of which waited for: 11 -> 7; matrix products, arithmetic and copies ran while one was open for 14% -> 5% of each run, Pallas kernels for 4% -> 1%
where the time goes in v1:
time: 669 us; the launch traced here: 675 us
  waiting for transfers between devices  276 us (41%)
  Pallas kernels  230 us (34%)
  local copies, waits for them, and re-layouts  44.3 us (7%)
  blocking collectives  41.2 us (6%)
  matrix products  34.8 us (5%)
  other arithmetic  20.1 us (3%)
  between operations  14.5 us (2%)
  starting transfers between devices  14.4 us (2%)
    reduce_scatter x2, waiting for transfers between devices, return_pairs(): lax.psum_scatter(both, 'grp', scatter_dimension=0, tiled=True)  101 us
    reduce_scatter x1, waiting for transfers between devices, reduce_grads(): mine = lax.psum_scatter(pack, 'wa', scatter_dimension=0, tiled=False)  95 us
    pallas_call x1, Pallas kernels, run_middle(): pl.pallas_call(functools.partial(middle_kernel, grp_count, wa_count, reac...  92.8 us
    psum x1, waiting for transfers between devices, reduce_grads(): total = lax.psum(mine, ('grp', 'pln')).astype(jnp.float32)  68.4 us
    pallas_call x1, Pallas kernels, run_opening(): pl.pallas_call(functools.partial(opening_kernel, grp_count, wa_count, rea...  48 us
    psum x1, blocking collectives, reduce_grads(): lax.psum(jnp.concatenate(vecs, axis=1).astype(jnp.bfloat16), ('grp', 'pln...  41.2 us
    pallas_call x5, Pallas kernels, run_swap(): pl.pallas_call(functools.partial(swap_kernel, inverse), out_shape=jax.Sha...  36.1 us
    pallas_call x2, Pallas kernels, attend_backward(): pl.pallas_call(functools.partial(backward_kernel, ranked), out_shape=(jax...  32.9 us
  transfers between devices with their start and end apart: 8, of which 7 were waited for; matrix products, arithmetic and copies ran while one was open for 5% of the time, Pallas kernels for 1%

profile of v1, /device:TPU:0, one launch (start us, length us, event | category | flops | bytes accessed | tf_op | source)
XLA Modules:
  0.0 675.3 jit_solution(14548696690930710586)
XLA Ops:
  7.3 4.3 concatenate.122
  12.2 48.0 %shard_map.510 = (bf16[512,512]{1,0:T(8,128)(2,1)}, bf16[512,512]{1,0:T(8,128)(2,1)}, bf16[512,512]{1,0:T(8,128)(2,1)}, bf16[512,512]{1,0:T(8,128)(2,1)}, bf16[5...) custom-call(bf16[256,512]{1,0:T(8,128)(2,1)} %bitcast.176, ...), custom_call_target="tpu_custom_call" | custom-call | tf_op jit(solution)/shard_map/pallas_call | solution.py:576
  64.3 2.0 fusion.42
  66.3 1.3 fusion.3
  68.7 1.5 fusion.63
  70.2 1.6 pad_maximum_fusion.2.km_ref
  72.7 9.6 %shard_map.511 = (f32[1024,128]{1,0:T(8,128)}, f32[1024,128]{1,0:T(8,128)}) custom-call(s32[1,4]{1,0:T(1,128)} %lens_ref.7, s32[1]{0:T(128)} %bitcast.own_ref, bf16[1024,128]{1,0:T(8,128)(2,1)} %get-tuple-element.58.q_ref, bf16[1024,128]{1,0:T(8,128)(2,1)} %pad_maximum_fusion.4.qm_ref, bf16[4096,128]{1,0:T(8,128)(2,1)} %get-tuple-element.118.k_ref, ...), custom_call_target="tpu_custom_call" | custom-call | tf_op jit(solution)/shard_map/pallas_call | solution.py:117
  82.3 92.8 %shard_map.512 = (f32[256,512]{1,0:T(8,128)}, f32[256,512]{1,0:T(8,128)}, f32[256,128]{1,0:T(8,128)}, bf16[256,512]{1,0:T(8,128)(2,1)}, bf16[1024,128]{1,0:T(8,1...) custom-call(f32[1024,128]{1,0:T(8,128)} %get-tuple-element.60.attended_ref.o_ref, ...), custom_call_target="tpu_custom_call" | custom-call | tf_op jit(solution)/shard_map/pallas_call | solution.py:652
  175.1 3.0 fusion.62
  178.1 1.6 pad_maximum_fusion.3.km_ref
  179.7 10.3 %shard_map.513 = (f32[1024,128]{1,0:T(8,128)}, f32[1024,128]{1,0:T(8,128)}) custom-call(s32[1,4]{1,0:T(1,128)} %lens_ref.7, s32[1]{0:T(128)} %bitcast.own_ref, bf16[1024,128]{1,0:T(8,128)(2,1)} %get-tuple-element.66.q_ref, bf16[1024,128]{1,0:T(8,128)(2,1)} %pad_maximum_fusion.5.qm_ref, bf16[4096,128]{1,0:T(8,128)(2,1)} %get-tuple-element.116.k_ref, ...), custom_call_target="tpu_custom_call" | custom-call | tf_op jit(solution)/shard_map/pallas_call | solution.py:117
  190.0 7.4 %shard_map.514 = bf16[256,512]{1,0:T(8,128)(2,1)} custom-call(f32[1024,128]{1,0:T(8,128)} %get-tuple-element.68.in_ref.o_ref), custom_call_target="tpu_custom_call" | custom-call | tf_op jit(solution)/shard_map/pallas_call | solution.py:690
  197.4 1.3 fusion.67
  199.0 5.1 fusion.6
  205.3 1.1 fusion.31
  206.6 1.4 fusion.69
  209.3 1.0 convolution_convert_fusion.11.in_ref
  210.3 7.1 %shard_map.515.do_ref = bf16[1024,128]{1,0:T(8,128)(2,1)} custom-call(bf16[256,512]{1,0:T(8,128)(2,1)} %convolution_convert_fusion.11.in_ref), custom_call_target="tpu_custom_call" | custom-call | tf_op jit(solution)/shard_map/pallas_call | solution.py:690
  217.5 16.7 %shard_map.516 = (bf16[1024,128]{1,0:T(8,128)(2,1)}, f32[4096,128]{1,0:T(8,128)}, f32[4096,128]{1,0:T(8,128)}) custom-call(s32[1,4]{1,0:T(1,128)} %lens_ref.7, s32[1]{0:T(128)} %bitcast.own_ref, bf16[1024,128]{1,0:T(8,128)(2,1)} %get-tuple-element.66.q_ref, bf16[1024,128]{1,0:T(8,128)(2,1)} %pad_maximum_fusion.5.qm_ref, ...), custom_call_target="tpu_custom_call" | custom-call | tf_op jit(solution)/shard_map/pallas_call | solution.py:200
  234.2 7.2 %shard_map.517 = bf16[256,512]{1,0:T(8,128)(2,1)} custom-call(bf16[1024,128]{1,0:T(8,128)(2,1)} %get-tuple-element.74.in_ref), custom_call_target="tpu_custom_call" | custom-call | tf_op jit(solution)/shard_map/pallas_call | solution.py:690
  241.4 1.5 multiply_reduce_fusion.1
  244.3 7.2 %shard_map.518.do_ref = bf16[1024,128]{1,0:T(8,128)(2,1)} custom-call(bf16[256,512]{1,0:T(8,128)(2,1)} %convolution_convert_fusion.10.in_ref), custom_call_target="tpu_custom_call" | custom-call | tf_op jit(solution)/shard_map/pallas_call | solution.py:690
  251.5 16.2 %shard_map.519 = (bf16[1024,128]{1,0:T(8,128)(2,1)}, f32[4096,128]{1,0:T(8,128)}, f32[4096,128]{1,0:T(8,128)}) custom-call(s32[1,4]{1,0:T(1,128)} %lens_ref.7, s32[1]{0:T(128)} %bitcast.own_ref, bf16[1024,128]{1,0:T(8,128)(2,1)} %get-tuple-element.58.q_ref, bf16[1024,128]{1,0:T(8,128)(2,1)} %pad_maximum_fusion.4.qm_ref, ...), custom_call_target="tpu_custom_call" | custom-call | tf_op jit(solution)/shard_map/pallas_call | solution.py:200
  267.7 1.8 convert.89
  270.1 1.6 pad_maximum_fusion
  271.8 1.8 convert.91
  274.0 1.5 pad_maximum_fusion.1
  275.6 7.2 %shard_map.520 = bf16[256,512]{1,0:T(8,128)(2,1)} custom-call(bf16[1024,128]{1,0:T(8,128)(2,1)} %get-tuple-element.77.in_ref), custom_call_target="tpu_custom_call" | custom-call | tf_op jit(solution)/shard_map/pallas_call | solution.py:690
  282.8 2.3 convolution_convert_fusion.1
  285.1 2.6 reshape.444
  287.6 1.4 convolution_convert_fusion.9
  289.8 1.1 convolution_convert_fusion.5
  291.0 1.1 convolution_convert_fusion.2
  292.1 1.1 convolution_convert_fusion.6
  294.0 61.2 %reduce-scatter.4.cloned.1.call-done = bf16[1024,256]{1,0:T(8,128)(2,1)} async-done(((bf16[4096,256]{1,0:T(8,128)(2,1)}), bf16[1024,256]{1,0:T(8,128)(2,1)}) %reduce-scatter.4.cloned.1.call-update) | async-done | bytes 524304 | tf_op jit(solution)/shard_map/reduce_scatter | solution.py:709
  355.1 1.1 fusion.65
  357.1 3.4 all-to-all-start
  361.3 40.0 %reduce-scatter.6.cloned.1.call-done = bf16[1024,256]{1,0:T(8,128)(2,1)} async-done(((bf16[4096,256]{1,0:T(8,128)(2,1)}), bf16[1024,256]{1,0:T(8,128)(2,1)}) %reduce-scatter.6.cloned.1.call-update) | async-done | bytes 524304 | tf_op jit(solution)/shard_map/reduce_scatter | solution.py:709
  401.3 1.8 fusion.64
  403.1 1.8 copy.61
  405.8 3.4 all-to-all-start.1
  409.2 2.1 convolution_convert_fusion.8
  411.3 3.9 all-to-all-done.1
  415.2 4.0 all-to-all-start.2
  419.2 2.1 convolution_convert_fusion.7
  421.3 4.0 all-to-all-done.2
  425.3 3.4 all-to-all-start.3
  428.8 2.2 convolution_convert_fusion.4
  430.9 3.8 all-to-all-done.3
  434.7 1.4 convolution_convert_fusion.3
  436.2 1.9 constant_dynamic-update-slice_fusion.8
  443.1 1.5 constant_dynamic-update-slice_fusion.1
  444.5 1.4 constant_dynamic-update-slice_fusion
  447.2 1.1 fusion.23
  448.8 95.0 %reduce-scatter.8.cloned.1.call-done = bf16[1,4096,512]{2,1,0:T(8,128)(2,1)} async-done(((bf16[2,4096,512]{2,1,0:T(8,128)(2,1)}), bf16[1,4096,512]{2,1,0:T(8,128)(2,1)}) %reduce-scatter.8.cloned.1.call-update) | async-done | bytes 4194320 | tf_op jit(solution)/shard_map/reduce_scatter | solution.py:718
  543.9 41.2 %psum.15 = bf16[2,4352]{1,0:T(2,128)(2,1)S(1)} all-reduce(bf16[2,4352]{1,0:T(2,128)(2,1)S(1)} %constant_dynamic-update-slice_fusion.10), channel_id=1, replica_groups=mesh['grp'=4,'pln'=4,'wa'=2] {'grp','pln','wa'}, use_global_device_ids=true, to_apply=%region_31.32 | all-reduce | flops 8704 | bytes 34816 | tf_op jit(solution)/shard_map/psum | solution.py:720
  585.7 1.4 fusion.70
  587.1 1.1 fusion.22
  588.3 1.3 fusion.71
  589.6 1.1 fusion.21
  591.4 68.4 %all-reduce.3.cloned.1.call-done = bf16[4096,512]{1,0:T(8,128)(2,1)} async-done(((bf16[4096,512]{1,0:T(8,128)(2,1)}), bf16[4096,512]{1,0:T(8,128)(2,1)}) %all-reduce.3.cloned.1.call-update) | async-done | bytes 4194320 | tf_op jit(solution)/shard_map/psum | solution.py:719
  659.8 3.5 fusion.60
  663.2 1.9 reshape.460
  665.2 3.6 fusion.61
  (175 shorter events, 24.1 us)
Async XLA Ops:
  7.2 54.5 %copy-start.36 = (s32[1,4]{1,0:T(1,128)S(1)}, s32[1,4]{1,0:T(1,128)}, u32[]{:S(2)}) copy-start(s32[1,4]{1,0:T(1,128)} %lens_ref.7) | copy-start | bytes 52
  7.2 57.1 %copy-start.35 = (s32[1,4096]{1,0:T(1,128)S(1)}, s32[1,4096]{1,0:T(1,128)}, u32[]{:S(2)}) copy-start(s32[1,4096]{1,0:T(1,128)} %param.36) | copy-start | bytes 49156
  7.2 347.9 %reduce-scatter.4.cloned.1.call-start = ((), (), s32[]{:S(2)}) async-start(), calls=%async_computation.7 | async-start | bytes 2621440 | tf_op jit(solution)/shard_map/reduce_scatter | solution.py:709
  66.3 2.4 copy-start.15
  179.7 17.7 %copy-start.22 = (f32[256,512]{1,0:T(8,128)S(1)}, f32[256,512]{1,0:T(8,128)}, u32[]{:S(2)}) copy-start(f32[256,512]{1,0:T(8,128)} %get-tuple-element.65) | copy-start | bytes 1572868
  179.7 17.7 %copy-start.24 = (bf16[512,512]{1,0:T(8,128)(2,1)S(1)}, bf16[512,512]{1,0:T(8,128)(2,1)}, u32[]{:S(2)}) copy-start(bf16[512,512]{1,0:T(8,128)(2,1)} %get-tuple-element.69) | copy-start | bytes 1572868
  190.0 9.1 %copy-start.37 = (bf16[512,2048]{1,0:T(8,128)(2,1)S(1)}, bf16[512,2048]{1,0:T(8,128)(2,1)}, u32[]{:S(2)}) copy-start(bf16[512,2048]{1,0:T(8,128)(2,1)} %get-tuple-element.70) | copy-start | bytes 6291460
  198.8 10.3 %copy-start.1 = (f32[256,512]{1,0:T(8,128)}, f32[256,512]{1,0:T(8,128)S(1)}, u32[]{:S(2)}) copy-start(f32[256,512]{1,0:T(8,128)S(1)} %get-tuple-element.157) | copy-start | bytes 1572868
  199.0 5.1 copy-start.38
  204.1 1.0 copy-start.26
  204.1 1.2 copy-start.8
  206.6 1.4 copy-start.11
  208.0 1.0 copy-start.28
  217.5 23.9 %copy-start.16 = (bf16[512,512]{1,0:T(8,128)(2,1)S(1)}, bf16[512,512]{1,0:T(8,128)(2,1)}, u32[]{:S(2)}) copy-start(bf16[512,512]{1,0:T(8,128)(2,1)} %get-tuple-element.62.query_mat_ref) | copy-start | bytes 1572868
  217.5 23.9 %copy-start.25 = (f32[256,512]{1,0:T(8,128)S(1)}, f32[256,512]{1,0:T(8,128)}, u32[]{:S(2)}) copy-start(f32[256,512]{1,0:T(8,128)} %get-tuple-element.75) | copy-start | bytes 1572868
  234.2 8.8 %copy-start.34 = (f32[256,128]{1,0:T(8,128)S(1)}, f32[256,128]{1,0:T(8,128)}, u32[]{:S(2)}) copy-start(f32[256,128]{1,0:T(8,128)} %get-tuple-element.72) | copy-start | bytes 393220
  241.4 1.9 copy-start.10
  267.7 2.2 copy-start.14
  271.7 2.2 copy-start.13
  271.7 129.6 %reduce-scatter.6.cloned.1.call-start = ((), (), s32[]{:S(2)}) async-start(), calls=%async_computation.8 | async-start | bytes 2621440 | tf_op jit(solution)/shard_map/reduce_scatter | solution.py:709
  285.0 2.6 copy-start.2
  287.6 2.2 copy-start.3
  287.6 2.2 copy-start.23
  287.6 3.3 copy-start.5
  289.0 3.1 copy-start.33
  289.8 3.4 copy-start.12
  289.8 3.4 copy-start.27
  357.1 48.7 %all-to-all-start = ((bf16[4,256,128]{1,2,0:T(8,128)(2,1)}), bf16[4,256,128]{1,2,0:T(8,128)(2,1)S(1)}, u32[]{:S(2)}, u32[]{:S(2)}) async-start(bf16[4,256,128]{1,2,0:T(8,128)(2,1)} %copy.59), calls=%async_computation.1 | async-start | bytes 524288 | tf_op jit(solution)/shard_map/all_to_all | solution.py:704
  405.7 19.6 %copy-start.6 = (bf16[4,256,128]{1,2,0:T(8,128)(2,1)}, bf16[4,256,128]{1,2,0:T(8,128)(2,1)S(1)}, u32[]{:S(2)}) copy-start(bf16[4,256,128]{1,2,0:T(8,128)(2,1)S(1)} %all-to-all-done) | copy-start | bytes 786436
  405.8 9.4 %all-to-all-start.1 = ((bf16[4,256,128]{1,2,0:T(8,128)(2,1)}), bf16[4,256,128]{1,2,0:T(8,128)(2,1)S(1)}, u32[]{:S(2)}, u32[]{:S(2)}) async-start(bf16[4,256,128]{1,2,0:T(8,128)(2,1)} %copy.60), calls=%async_computation.2 | async-start | bytes 524288 | tf_op jit(solution)/shard_map/all_to_all | solution.py:704
  415.2 10.1 %all-to-all-start.2 = ((bf16[4,256,128]{1,2,0:T(8,128)(2,1)}), bf16[4,256,128]{1,2,0:T(8,128)(2,1)}, u32[]{:S(2)}, u32[]{:S(2)}) async-start(bf16[4,256,128]{1,2,0:T(8,128)(2,1)} %copy.61), calls=%async_computation.4 | async-start | bytes 524288 | tf_op jit(solution)/shard_map/all_to_all | solution.py:704
  425.3 9.4 %all-to-all-start.3 = ((bf16[4,256,128]{1,2,0:T(8,128)(2,1)}), bf16[4,256,128]{1,2,0:T(8,128)(2,1)S(1)}, u32[]{:S(2)}, u32[]{:S(2)}) async-start(bf16[4,256,128]{1,2,0:T(8,128)(2,1)} %copy.62), calls=%async_computation.5 | async-start | bytes 524288 | tf_op jit(solution)/shard_map/all_to_all | solution.py:704
  428.7 115.0 %reduce-scatter.8.cloned.1.call-start = ((), (), s32[]{:S(2)}) async-start(), calls=%async_computation.9 | async-start | bytes 12582912 | tf_op jit(solution)/shard_map/reduce_scatter | solution.py:718
  434.7 3.3 copy-start.20
  434.7 4.2 copy-start.19
  434.7 5.0 copy-start.18
  436.1 4.4 copy-start.21
  438.9 3.3 copy-start.17
  439.7 3.3 copy-start
  445.9 0.9 copy-start.4
  445.9 1.0 copy-start.9
  445.9 1.3 copy-start.31
  446.0 213.8 %all-reduce.3.cloned.1.call-start = ((), (), s32[]{:S(2)}) async-start(), calls=%async_computation.10 | async-start | bytes 8388608 | tf_op jit(solution)/shard_map/psum | solution.py:719
  543.8 41.9 %copy-start.7 = (bf16[4,256,128]{1,2,0:T(8,128)(2,1)S(1)}, bf16[4,256,128]{1,2,0:T(8,128)(2,1)}, u32[]{:S(2)}) copy-start(bf16[4,256,128]{1,2,0:T(8,128)(2,1)} %copy-done.6) | copy-start | bytes 786436
  543.8 43.4 %copy-start.30 = (bf16[512,512]{1,0:T(8,128)(2,1)S(1)}, bf16[512,512]{1,0:T(8,128)(2,1)}, u32[]{:S(2)}) copy-start(bf16[512,512]{1,0:T(8,128)(2,1)} %get-tuple-element.82) | copy-start | bytes 1572868
  543.8 44.5 %copy-start.32 = (bf16[512,512]{1,0:T(8,128)(2,1)S(1)}, bf16[512,512]{1,0:T(8,128)(2,1)}, u32[]{:S(2)}) copy-start(bf16[512,512]{1,0:T(8,128)(2,1)} %get-tuple-element.85) | copy-start | bytes 1572868
  585.7 3.9 copy-start.29
Sparse Core Ops, SparseCore 0:
  271.8 83.2 reduce-scatter.3
  358.1 43.1 reduce-scatter.5
  446.1 97.6 reduce-scatter.7
  547.8 111.9 all-reduce.2
